TPU v7x, 256 devices: a whole 4x4x8 slice. The times are simulated.
256 devices in a mesh: row: 16 (over z, core), col: 16 (over y, x).
Axes of the slice: x: 4, y: 4, z: 8, core: 2. Of those that a mesh axis runs over, the one named last changes fastest.
Arguments:
- right_sides: float32 [4, 1024, 4096], P(None, 'row', 'col'), may hold values from -6 to 6
- low_left: bfloat16 [6, 4096, 128], P(None, 'col'), may hold values from -0.25 to 0.25
- low_right: bfloat16 [6, 4096, 128], P(None, 'col'), may hold values from -0.09375 to 0.09375
- up_left: bfloat16 [6, 4096, 128], P(None, 'col'), may hold values from -0.25 to 0.25
- up_right: bfloat16 [6, 4096, 128], P(None, 'col'), may hold values from -0.09375 to 0.09375
- low_ranks: int32 [6], replicated, may hold values from 1 to 4
- up_ranks: int32 [6], replicated, may hold values from 1 to 4
- inv_lower: bfloat16 [4, 4096, 4096], P(None, 'col', 'row'), may hold values from -0.09375 to 0.09375
- inv_upper: bfloat16 [4, 4096, 4096], P(None, 'col', 'row'), may hold values from -0.09375 to 0.09375
Outputs:
- solution: float32 [4, 1024, 4096], P(None, 'row', 'col')
Inputs may be any that keep to these rules, and one draw needn't show every extreme that they name: `low_ranks`: factor columns beyond 32 times this value are padding with arbitrary values and must be masked out. `up_ranks`: factor columns beyond 32 times this value are padding with arbitrary values and must be masked out.
All inputs are finite; a program needn't handle non-finite values.
Results may differ from a plain program's by a relative error of at most 0.03.
Values may be sent and summed in bfloat16 or wider, within the bound.
No kernel may reach another device: no remote copies, remote signals or barrier semaphores. Data moves between devices by JAX's collectives and lax.ppermute only.
A program may use at most 64 MiB of HBM per device.

v0:
```python
import jax
import jax.numpy as jnp
import numpy as np
from jax import lax
from jax.sharding import PartitionSpec as P

RBLK = 32


def laid_out(parts, dim):
    parts = jnp.moveaxis(parts, 0, dim)
    lengths = parts.shape
    return parts.reshape(*lengths[:dim], lengths[dim] * lengths[dim + 1], *lengths[dim + 2 :])


def from_everyone(value, axis):
    length = lax.axis_size(axis)
    return lax.all_to_all(
        jnp.broadcast_to(value[None], (length, *value.shape)), axis, 0, 0, tiled=True
    )


def gathered_copies(value, axis, dim):
    return laid_out(from_everyone(value, axis), dim)


def of_everyone(value, axis):
    everything = from_everyone(value, axis)
    return jnp.sum(everything.astype(jnp.float32), axis=0)


def rank_mask(ranks, pair_index, rank_cols):
    columns = jnp.arange(rank_cols, dtype=jnp.int32)
    return (columns[None, :] < RBLK * ranks[pair_index][:, None]).astype(jnp.float32)


def times_inverse(block, inverse):
    return lax.dot_general(
        block, inverse, (((1,), (1,)), ((), ())), preferred_element_type=jnp.float32
    )


def fold_columns(whole, piece):
    return times_inverse(whole, piece)


def shards(
    right_sides, low_left, low_right, up_left, up_right, low_ranks, up_ranks, inv_lower, inv_upper
):
    tile_count = right_sides.shape[0]
    rank_cols = low_left.shape[2]
    residual = right_sides
    forward = []
    for section in range(tile_count):
        rounded = residual[section].astype(jnp.bfloat16)
        whole = gathered_copies(rounded, "col", 1)
        solved = fold_columns(whole, lax.all_gather(inv_lower[section], "row", axis=1, tiled=True))
        forward.append(solved)
        if section + 1 < tile_count:
            pair_index = np.array(
                [tile * (tile - 1) // 2 + section for tile in range(section + 1, tile_count)],
                dtype=np.int32,
            )
            projections = jnp.einsum(
                "nw,mwr->mnr",
                solved.astype(jnp.bfloat16),
                low_right[pair_index],
                preferred_element_type=jnp.float32,
            )
            summed = of_everyone(projections.astype(jnp.bfloat16), "col").astype(jnp.float32)
            masked = (summed * rank_mask(low_ranks, pair_index, rank_cols)[:, None, :]).astype(
                jnp.bfloat16
            )
            update = jnp.einsum(
                "mnr,mwr->mnw", masked, low_left[pair_index], preferred_element_type=jnp.float32
            )
            residual = residual.at[section + 1 :].add(-update)
    state = jnp.stack(forward)
    solutions = [None] * tile_count
    for section in range(tile_count - 1, -1, -1):
        rounded = state[section].astype(jnp.bfloat16)
        whole = gathered_copies(rounded, "col", 1)
        solved = fold_columns(whole, lax.all_gather(inv_upper[section], "row", axis=1, tiled=True))
        solutions[section] = solved
        if section > 0:
            pair_index = np.array(
                [section * (section - 1) // 2 + tile for tile in range(section)], dtype=np.int32
            )
            projections = jnp.einsum(
                "nw,mwr->mnr",
                solved.astype(jnp.bfloat16),
                up_right[pair_index],
                preferred_element_type=jnp.float32,
            )
            summed = of_everyone(projections.astype(jnp.bfloat16), "col").astype(jnp.float32)
            masked = (summed * rank_mask(up_ranks, pair_index, rank_cols)[:, None, :]).astype(
                jnp.bfloat16
            )
            update = jnp.einsum(
                "mnr,mwr->mnw", masked, up_left[pair_index], preferred_element_type=jnp.float32
            )
            state = state.at[:section].add(-update)
    return jnp.stack(solutions)


def solution(mesh):
    in_specs = (
        P(None, "row", "col"),
        P(None, "col", None),
        P(None, "col", None),
        P(None, "col", None),
        P(None, "col", None),
        P(),
        P(),
        P(None, "col", "row"),
        P(None, "col", "row"),
    )
    out_specs = P(None, "row", "col")
    return jax.shard_map(shards, mesh=mesh, in_specs=in_specs, out_specs=out_specs, check_vma=False)
```

profile of v0, /device:TPU:1, one launch (start us, length us, event | category | flops | bytes accessed | tf_op | source)
XLA Modules:
  0.0 357.1 jit_solution(16431836217036689485)
XLA Ops:
  13.4 7.6 %all-to-all-start = ((bf16[16,64,256]{2,1,0:T(8,128)(2,1)}), bf16[16,64,256]{2,1,0:T(8,128)(2,1)S(1)}, u32[]{:S(2)}, u32[]{:S(2)}) async-start(bf16[16,64,256]{2,1,0:T(8,128)(2,1)} %broadcast_in_dim.83), calls=%async_computation | async-start | bytes 1048576 | tf_op jit(solution)/shard_map/all_to_all | solution.py:18
  21.6 9.9 %all-to-all-done = bf16[16,64,256]{2,1,0:T(8,128)(2,1)S(1)} async-done(((bf16[16,64,256]{2,1,0:T(8,128)(2,1)}), bf16[16,64,256]{2,1,0:T(8,128)(2,1)S(1)}, u32[]{:S(2)}, u32[]{:S(2)}) %all-to-all-start) | async-done | bytes 524320 | tf_op jit(solution)/shard_map/all_to_all | solution.py:18
  31.6 22.7 %all-gather.17.cloned.1.call-done = bf16[1,256,4096]{2,1,0:T(8,128)(2,1)} async-done(((bf16[1,256,256]{2,1,0:T(8,128)(2,1)}), bf16[1,256,4096]{2,1,0:T(8,128)(2,1)}) %all-gather.17.cloned.1.call-update) | async-done | bytes 2097168 | tf_op jit(solution)/shard_map/all_gather | solution.py:57
  57.9 6.5 %all-to-all-start.1 = ((bf16[16,3,64,128]{3,2,1,0:T(8,128)(2,1)}), bf16[16,3,64,128]{3,2,1,0:T(8,128)(2,1)S(1)}, u32[]{:S(2)}, u32[]{:S(2)}) async-start(bf16[16,3,64,128]{3,2,1,0:T(8,128)(2,1)} %broadcast_in_dim.85), calls=%async_computation.1 | async-start | bytes 1572864 | tf_op jit(solution)/shard_map/all_to_all | solution.py:18
  66.4 11.7 %all-to-all-done.1 = bf16[16,3,64,128]{3,2,1,0:T(8,128)(2,1)S(1)} async-done(((bf16[16,3,64,128]{3,2,1,0:T(8,128)(2,1)}), bf16[16,3,64,128]{3,2,1,0:T(8,128)(2,1)S(1)}, u32[]{:S(2)}, u32[]{:S(2)}) %all-to-all-start.1) | async-done | bytes 786464 | tf_op jit(solution)/shard_map/all_to_all | solution.py:18
  83.5 9.5 %all-to-all-done.2 = bf16[16,64,256]{2,1,0:T(8,128)(2,1)S(1)} async-done(((bf16[16,64,256]{2,1,0:T(8,128)(2,1)}), bf16[16,64,256]{2,1,0:T(8,128)(2,1)S(1)}, u32[]{:S(2)}, u32[]{:S(2)}) %all-to-all-start.2) | async-done | bytes 524320 | tf_op jit(solution)/shard_map/all_to_all | solution.py:18
  107.5 9.5 %all-to-all-done.3 = bf16[16,2,64,128]{3,2,1,0:T(8,128)(2,1)S(1)} async-done(((bf16[16,2,64,128]{3,2,1,0:T(8,128)(2,1)}), bf16[16,2,64,128]{3,2,1,0:T(8,128)(2,1)S(1)}, u32[]{:S(2)}, u32[]{:S(2)}) %all-to-all-start.3) | async-done | bytes 524320 | tf_op jit(solution)/shard_map/all_to_all | solution.py:18
  122.4 9.3 %all-to-all-done.4 = bf16[16,64,256]{2,1,0:T(8,128)(2,1)S(1)} async-done(((bf16[16,64,256]{2,1,0:T(8,128)(2,1)}), bf16[16,64,256]{2,1,0:T(8,128)(2,1)S(1)}, u32[]{:S(2)}, u32[]{:S(2)}) %all-to-all-start.4) | async-done | bytes 524320 | tf_op jit(solution)/shard_map/all_to_all | solution.py:18
  141.3 6.5 %all-to-all-start.5 = ((bf16[16,1,64,128]{3,2,1,0:T(8,128)(2,1)}), bf16[16,1,64,128]{3,2,1,0:T(8,128)(2,1)S(1)}, u32[]{:S(2)}, u32[]{:S(2)}) async-start(bf16[16,1,64,128]{3,2,1,0:T(8,128)(2,1)} %broadcast_in_dim.191), calls=%async_computation.5 | async-start | bytes 524288 | tf_op jit(solution)/shard_map/all_to_all | solution.py:18
  149.0 7.1 %all-to-all-done.5 = bf16[16,1,64,128]{3,2,1,0:T(8,128)(2,1)S(1)} async-done(((bf16[16,1,64,128]{3,2,1,0:T(8,128)(2,1)}), bf16[16,1,64,128]{3,2,1,0:T(8,128)(2,1)S(1)}, u32[]{:S(2)}, u32[]{:S(2)}) %all-to-all-start.5) | async-done | bytes 262176 | tf_op jit(solution)/shard_map/all_to_all | solution.py:18
  156.3 12.8 %all_to_all.70 = bf16[16,64,256]{2,1,0:T(8,128)(2,1)S(1)} all-to-all(bf16[16,64,256]{2,1,0:T(8,128)(2,1)S(1)} %broadcast_in_dim.195), channel_id=1, replica_groups=mesh['row'=16,'col'=16] {'col'}, dimensions={0} | all-to-all | bytes 1048576 | tf_op jit(solution)/shard_map/all_to_all | solution.py:18
  169.2 10.6 %all-gather.23.cloned.1.call-done = bf16[1,256,4096]{2,1,0:T(8,128)(2,1)} async-done(((bf16[1,256,256]{2,1,0:T(8,128)(2,1)}), bf16[1,256,4096]{2,1,0:T(8,128)(2,1)}) %all-gather.23.cloned.1.call-update) | async-done | bytes 2097168 | tf_op jit(solution)/shard_map/all_gather | solution.py:57
  190.2 10.2 %all-to-all-done.7 = bf16[16,64,256]{2,1,0:T(8,128)(2,1)S(1)} async-done(((bf16[16,64,256]{2,1,0:T(8,128)(2,1)}), bf16[16,64,256]{2,1,0:T(8,128)(2,1)S(1)}, u32[]{:S(2)}, u32[]{:S(2)}) %all-to-all-start.7) | async-done | bytes 524320 | tf_op jit(solution)/shard_map/all_to_all | solution.py:18
  200.5 21.2 %all-gather.25.cloned.1.call-done = bf16[1,256,4096]{2,1,0:T(8,128)(2,1)} async-done(((bf16[1,256,256]{2,1,0:T(8,128)(2,1)}), bf16[1,256,4096]{2,1,0:T(8,128)(2,1)}) %all-gather.25.cloned.1.call-update) | async-done | bytes 2097168 | tf_op jit(solution)/shard_map/all_gather | solution.py:83
  225.3 6.5 %all-to-all-start.8 = ((bf16[16,3,64,128]{3,2,1,0:T(8,128)(2,1)}), bf16[16,3,64,128]{3,2,1,0:T(8,128)(2,1)S(1)}, u32[]{:S(2)}, u32[]{:S(2)}) async-start(bf16[16,3,64,128]{3,2,1,0:T(8,128)(2,1)} %broadcast_in_dim.197), calls=%async_computation.8 | async-start | bytes 1572864 | tf_op jit(solution)/shard_map/all_to_all | solution.py:18
  233.2 12.3 %all-to-all-done.8 = bf16[16,3,64,128]{3,2,1,0:T(8,128)(2,1)S(1)} async-done(((bf16[16,3,64,128]{3,2,1,0:T(8,128)(2,1)}), bf16[16,3,64,128]{3,2,1,0:T(8,128)(2,1)S(1)}, u32[]{:S(2)}, u32[]{:S(2)}) %all-to-all-start.8) | async-done | bytes 786464 | tf_op jit(solution)/shard_map/all_to_all | solution.py:18
  251.6 8.8 %all-to-all-done.9 = bf16[16,64,256]{2,1,0:T(8,128)(2,1)S(1)} async-done(((bf16[16,64,256]{2,1,0:T(8,128)(2,1)}), bf16[16,64,256]{2,1,0:T(8,128)(2,1)S(1)}, u32[]{:S(2)}, u32[]{:S(2)}) %all-to-all-start.9) | async-done | bytes 524320 | tf_op jit(solution)/shard_map/all_to_all | solution.py:18
  266.8 6.5 %all-to-all-start.10 = ((bf16[16,2,64,128]{3,2,1,0:T(8,128)(2,1)}), bf16[16,2,64,128]{3,2,1,0:T(8,128)(2,1)S(1)}, u32[]{:S(2)}, u32[]{:S(2)}) async-start(bf16[16,2,64,128]{3,2,1,0:T(8,128)(2,1)} %broadcast_in_dim.203), calls=%async_computation.10 | async-start | bytes 1048576 | tf_op jit(solution)/shard_map/all_to_all | solution.py:18
  274.7 9.5 %all-to-all-done.10 = bf16[16,2,64,128]{3,2,1,0:T(8,128)(2,1)S(1)} async-done(((bf16[16,2,64,128]{3,2,1,0:T(8,128)(2,1)}), bf16[16,2,64,128]{3,2,1,0:T(8,128)(2,1)S(1)}, u32[]{:S(2)}, u32[]{:S(2)}) %all-to-all-start.10) | async-done | bytes 524320 | tf_op jit(solution)/shard_map/all_to_all | solution.py:18
  284.5 13.4 %all_to_all.71 = bf16[16,64,256]{2,1,0:T(8,128)(2,1)S(1)} all-to-all(bf16[16,64,256]{2,1,0:T(8,128)(2,1)S(1)} %broadcast_in_dim.208), channel_id=1, replica_groups=mesh['row'=16,'col'=16] {'col'}, dimensions={0} | all-to-all | bytes 1048576 | tf_op jit(solution)/shard_map/all_to_all | solution.py:18
  297.9 7.4 %all-gather.29.cloned.1.call-done = bf16[1,256,4096]{2,1,0:T(8,128)(2,1)} async-done(((bf16[1,256,256]{2,1,0:T(8,128)(2,1)}), bf16[1,256,4096]{2,1,0:T(8,128)(2,1)}) %all-gather.29.cloned.1.call-update) | async-done | bytes 2097168 | tf_op jit(solution)/shard_map/all_gather | solution.py:83
  315.1 8.2 %all-to-all-done.12 = bf16[16,1,64,128]{3,2,1,0:T(8,128)(2,1)S(1)} async-done(((bf16[16,1,64,128]{3,2,1,0:T(8,128)(2,1)}), bf16[16,1,64,128]{3,2,1,0:T(8,128)(2,1)S(1)}, u32[]{:S(2)}, u32[]{:S(2)}) %all-to-all-start.12) | async-done | bytes 262176 | tf_op jit(solution)/shard_map/all_to_all | solution.py:18
  323.5 12.8 %all_to_all.72 = bf16[16,64,256]{2,1,0:T(8,128)(2,1)S(1)} all-to-all(bf16[16,64,256]{2,1,0:T(8,128)(2,1)S(1)} %broadcast_in_dim.214), channel_id=1, replica_groups=mesh['row'=16,'col'=16] {'col'}, dimensions={0} | all-to-all | bytes 1048576 | tf_op jit(solution)/shard_map/all_to_all | solution.py:18
  336.4 10.8 %all-gather.31.cloned.1.call-done = bf16[1,256,4096]{2,1,0:T(8,128)(2,1)} async-done(((bf16[1,256,256]{2,1,0:T(8,128)(2,1)}), bf16[1,256,4096]{2,1,0:T(8,128)(2,1)}) %all-gather.31.cloned.1.call-update) | async-done | bytes 2097168 | tf_op jit(solution)/shard_map/all_gather | solution.py:83
  (130 shorter events, 91.2 us)
Async XLA Ops:
  6.5 14.5 %copy-start.10 = (s32[3]{0:T(128)S(1)}, s32[3]{0:T(128)}, u32[]{:S(2)}) copy-start(s32[3]{0:T(128)} %constant.313) | copy-start | bytes 40
  6.5 14.5 %copy-start.2 = (bf16[6,256,128]{2,1,0:T(8,128)(2,1)S(1)}, bf16[6,256,128]{2,1,0:T(8,128)(2,1)}, u32[]{:S(2)}) copy-start(bf16[6,256,128]{2,1,0:T(8,128)(2,1)} %param.47) | copy-start | bytes 1179652
  6.5 47.7 %all-gather.17.cloned.1.call-start = ((), (), s32[]{:S(2)}) async-start(), calls=%async_computation.14 | async-start | bytes 2228224 | tf_op jit(solution)/shard_map/all_gather | solution.py:57
  8.5 87.7 %all-gather.19.cloned.1.call-start = ((), (), s32[]{:S(2)}) async-start(), calls=%async_computation.15 | async-start | bytes 2228224 | tf_op jit(solution)/shard_map/all_gather | solution.py:57
  9.3 128.8 %all-gather.21.cloned.1.call-start = ((), (), s32[]{:S(2)}) async-start(), calls=%async_computation.16 | async-start | bytes 2228224 | tf_op jit(solution)/shard_map/all_gather | solution.py:57
  10.0 169.8 %all-gather.23.cloned.1.call-start = ((), (), s32[]{:S(2)}) async-start(), calls=%async_computation.17 | async-start | bytes 2228224 | tf_op jit(solution)/shard_map/all_gather | solution.py:57
  10.6 211.0 %all-gather.25.cloned.1.call-start = ((), (), s32[]{:S(2)}) async-start(), calls=%async_computation.18 | async-start | bytes 2228224 | tf_op jit(solution)/shard_map/all_gather | solution.py:83
  13.4 18.1 %all-to-all-start = ((bf16[16,64,256]{2,1,0:T(8,128)(2,1)}), bf16[16,64,256]{2,1,0:T(8,128)(2,1)S(1)}, u32[]{:S(2)}, u32[]{:S(2)}) async-start(bf16[16,64,256]{2,1,0:T(8,128)(2,1)} %broadcast_in_dim.83), calls=%async_computation | async-start | bytes 1048576 | tf_op jit(solution)/shard_map/all_to_all | solution.py:18
  57.9 20.2 %all-to-all-start.1 = ((bf16[16,3,64,128]{3,2,1,0:T(8,128)(2,1)}), bf16[16,3,64,128]{3,2,1,0:T(8,128)(2,1)S(1)}, u32[]{:S(2)}, u32[]{:S(2)}) async-start(bf16[16,3,64,128]{3,2,1,0:T(8,128)(2,1)} %broadcast_in_dim.85), calls=%async_computation.1 | async-start | bytes 1572864 | tf_op jit(solution)/shard_map/all_to_all | solution.py:18
  64.4 198.9 %all-gather.27.cloned.1.call-start = ((), (), s32[]{:S(2)}) async-start(), calls=%async_computation.19 | async-start | bytes 2228224 | tf_op jit(solution)/shard_map/all_gather | solution.py:83
  65.0 17.9 %copy-start.9 = (s32[2]{0:T(128)S(1)}, s32[2]{0:T(128)}, u32[]{:S(2)}) copy-start(s32[2]{0:T(128)} %constant.316) | copy-start | bytes 28
  79.3 13.8 %all-to-all-start.2 = ((bf16[16,64,256]{2,1,0:T(8,128)(2,1)}), bf16[16,64,256]{2,1,0:T(8,128)(2,1)S(1)}, u32[]{:S(2)}, u32[]{:S(2)}) async-start(bf16[16,64,256]{2,1,0:T(8,128)(2,1)} %broadcast_in_dim.89), calls=%async_computation.2 | async-start | bytes 1048576 | tf_op jit(solution)/shard_map/all_to_all | solution.py:18
  99.7 17.4 %all-to-all-start.3 = ((bf16[16,2,64,128]{3,2,1,0:T(8,128)(2,1)}), bf16[16,2,64,128]{3,2,1,0:T(8,128)(2,1)S(1)}, u32[]{:S(2)}, u32[]{:S(2)}) async-start(bf16[16,2,64,128]{3,2,1,0:T(8,128)(2,1)} %broadcast_in_dim.91), calls=%async_computation.3 | async-start | bytes 1048576 | tf_op jit(solution)/shard_map/all_to_all | solution.py:18
  118.1 13.6 %all-to-all-start.4 = ((bf16[16,64,256]{2,1,0:T(8,128)(2,1)}), bf16[16,64,256]{2,1,0:T(8,128)(2,1)S(1)}, u32[]{:S(2)}, u32[]{:S(2)}) async-start(bf16[16,64,256]{2,1,0:T(8,128)(2,1)} %broadcast_in_dim.187), calls=%async_computation.4 | async-start | bytes 1048576 | tf_op jit(solution)/shard_map/all_to_all | solution.py:18
  121.7 183.6 %all-gather.29.cloned.1.call-start = ((), (), s32[]{:S(2)}) async-start(), calls=%async_computation.20 | async-start | bytes 2228224 | tf_op jit(solution)/shard_map/all_gather | solution.py:83
  141.3 14.8 %all-to-all-start.5 = ((bf16[16,1,64,128]{3,2,1,0:T(8,128)(2,1)}), bf16[16,1,64,128]{3,2,1,0:T(8,128)(2,1)S(1)}, u32[]{:S(2)}, u32[]{:S(2)}) async-start(bf16[16,1,64,128]{3,2,1,0:T(8,128)(2,1)} %broadcast_in_dim.191), calls=%async_computation.5 | async-start | bytes 524288 | tf_op jit(solution)/shard_map/all_to_all | solution.py:18
  183.1 17.4 %all-to-all-start.7 = ((bf16[16,64,256]{2,1,0:T(8,128)(2,1)}), bf16[16,64,256]{2,1,0:T(8,128)(2,1)S(1)}, u32[]{:S(2)}, u32[]{:S(2)}) async-start(bf16[16,64,256]{2,1,0:T(8,128)(2,1)} %broadcast_in_dim.196), calls=%async_computation.7 | async-start | bytes 1048576 | tf_op jit(solution)/shard_map/all_to_all | solution.py:18
  221.6 10.2 %copy-start.5 = (bf16[6,256,128]{2,1,0:T(8,128)(2,1)S(1)}, bf16[6,256,128]{2,1,0:T(8,128)(2,1)}, u32[]{:S(2)}) copy-start(bf16[6,256,128]{2,1,0:T(8,128)(2,1)} %param.48) | copy-start | bytes 1179652
  225.3 20.2 %all-to-all-start.8 = ((bf16[16,3,64,128]{3,2,1,0:T(8,128)(2,1)}), bf16[16,3,64,128]{3,2,1,0:T(8,128)(2,1)S(1)}, u32[]{:S(2)}, u32[]{:S(2)}) async-start(bf16[16,3,64,128]{3,2,1,0:T(8,128)(2,1)} %broadcast_in_dim.197), calls=%async_computation.8 | async-start | bytes 1572864 | tf_op jit(solution)/shard_map/all_to_all | solution.py:18
  231.8 19.2 %copy-start.7 = (s32[2]{0:T(128)S(1)}, s32[2]{0:T(128)}, u32[]{:S(2)}) copy-start(s32[2]{0:T(128)} %constant.322) | copy-start | bytes 28
  246.6 13.8 %all-to-all-start.9 = ((bf16[16,64,256]{2,1,0:T(8,128)(2,1)}), bf16[16,64,256]{2,1,0:T(8,128)(2,1)S(1)}, u32[]{:S(2)}, u32[]{:S(2)}) async-start(bf16[16,64,256]{2,1,0:T(8,128)(2,1)} %broadcast_in_dim.202), calls=%async_computation.9 | async-start | bytes 1048576 | tf_op jit(solution)/shard_map/all_to_all | solution.py:18
  250.3 96.9 %all-gather.31.cloned.1.call-start = ((), (), s32[]{:S(2)}) async-start(), calls=%async_computation.21 | async-start | bytes 2228224 | tf_op jit(solution)/shard_map/all_gather | solution.py:83
  266.8 17.4 %all-to-all-start.10 = ((bf16[16,2,64,128]{3,2,1,0:T(8,128)(2,1)}), bf16[16,2,64,128]{3,2,1,0:T(8,128)(2,1)S(1)}, u32[]{:S(2)}, u32[]{:S(2)}) async-start(bf16[16,2,64,128]{3,2,1,0:T(8,128)(2,1)} %broadcast_in_dim.203), calls=%async_computation.10 | async-start | bytes 1048576 | tf_op jit(solution)/shard_map/all_to_all | solution.py:18
  308.5 14.7 %all-to-all-start.12 = ((bf16[16,1,64,128]{3,2,1,0:T(8,128)(2,1)}), bf16[16,1,64,128]{3,2,1,0:T(8,128)(2,1)S(1)}, u32[]{:S(2)}, u32[]{:S(2)}) async-start(bf16[16,1,64,128]{3,2,1,0:T(8,128)(2,1)} %broadcast_in_dim.210), calls=%async_computation.12 | async-start | bytes 524288 | tf_op jit(solution)/shard_map/all_to_all | solution.py:18
  (6 other events, 51.4 us)
Sparse Core Ops, SparseCore 0:
  9.1 45.1 all-gather.16
  56.0 40.1 all-gather.18
  98.0 40.0 all-gather.20
  139.7 40.0 all-gather.22
  181.4 40.1 all-gather.24
  223.2 40.1 all-gather.26
  265.1 40.0 all-gather.28
  307.0 40.0 all-gather.30
where the time goes:
time: 359 us; the launch traced here: 357 us
  waiting for transfers between devices  195 us (54%)
  starting transfers between devices  64.4 us (18%)
  blocking collectives  39 us (11%)
  local copies, waits for them, and re-layouts  21.9 us (6%)
  matrix products  20.8 us (6%)
  between operations  14.5 us (4%)
    all_to_all x11, waiting for transfers between devices, from_everyone(): lax.all_to_all(jnp.broadcast_to(value[None], (length, *value.shape)), axi...  106 us
    all_to_all x11, starting transfers between devices, from_everyone(): lax.all_to_all(jnp.broadcast_to(value[None], (length, *value.shape)), axi...  64.1 us
    all_gather x4, waiting for transfers between devices, shards(): lax.all_gather(inv_lower[section], 'row', axis=1, tiled=True)  42.8 us
    all_gather x4, waiting for transfers between devices, shards(): lax.all_gather(inv_upper[section], 'row', axis=1, tiled=True)  42.2 us
    all_to_all x3, blocking collectives, from_everyone(): lax.all_to_all(jnp.broadcast_to(value[None], (length, *value.shape)), axi...  39 us
    dot_general x8, matrix products, times_inverse(): lax.dot_general(block, inverse, (((1,), (1,)), ((), ())), preferred_eleme...  18.9 us
    broadcast_in_dim x19, local copies, waits for them, and re-layouts, from_everyone(): jnp.broadcast_to(value[None], (length, *value.shape))  9.98 us
  transfers between devices with their start and end apart: 19, of which 19 were waited for; matrix products, arithmetic and copies ran while one was open for 11% of the time, Pallas kernels for 0%

commit v1 on v0

--- a/solution.py
+++ b/solution.py
@@ -80,7 +80,27 @@
     for section in range(tile_count - 1, -1, -1):
         rounded = state[section].astype(jnp.bfloat16)
         whole = gathered_copies(rounded, "col", 1)
-        solved = fold_columns(whole, lax.all_gather(inv_upper[section], "row", axis=1, tiled=True))
+
+        def wires_group(ax_name, tile_in):
+            n_slots = lax.axis_size(ax_name)
+            entries = []
+            for to_i in range(n_slots):
+                entries.append((to_i, (to_i + 1) % n_slots))
+            row_list = []
+            for to_i in range(n_slots):
+                row_list.append((to_i, (to_i - 1) % n_slots))
+            reply, tmp = ([tile_in], [tile_in])
+            for _ in range(n_slots // 2):
+                reply.append(lax.ppermute(reply[-1], ax_name, entries))
+            for _ in range((n_slots - 1) // 2):
+                v_now = lax.ppermute(tmp[-1], ax_name, row_list)
+                tmp.append(v_now)
+            moved = jnp.concatenate([*reply[::-1], *tmp[1:]], axis=1)
+            return jnp.roll(
+                moved, (lax.axis_index(ax_name) - n_slots // 2) * tile_in.shape[1], axis=1
+            )
+
+        solved = fold_columns(whole, wires_group("row", inv_upper[section]))
         solutions[section] = solved
         if section > 0:
             pair_index = np.array(

time: 359 us -> 343 us (0.955)
  waiting for transfers between devices: 195 us -> 46.5 us
  starting transfers between devices: 64.4 us -> 155 us
  local copies, waits for them, and re-layouts: 21.9 us -> 97.5 us
  blocking collectives: 39 us -> 0 us
    ppermute x0 -> x60, starting transfers between devices: none -> 83.2 us  [the longest x28 52.3 us: wires_group(): v_now = lax.ppermute(tmp[-1], ax_name, row_list)]
    unnamed x22 -> x153, local copies, waits for them, and re-layouts: 0.05 us -> 67.4 us
    all_to_all x11 -> x14, waiting for transfers between devices: 106 us -> 39.1 us  [from_everyone(): lax.all_to_all(jnp.broadcast_to(value[None], (length, *value.shape)), axi...]
    all_gather x4, waiting for transfers between devices: 42.8 us -> 0.06 us  [shards(): lax.all_gather(inv_lower[section], 'row', axis=1, tiled=True)]
    all_gather x4 -> x0, waiting for transfers between devices: 42.2 us -> none  [shards(): lax.all_gather(inv_upper[section], 'row', axis=1, tiled=True)]
    all_to_all x3 -> x0, blocking collectives: 39 us -> none  [from_everyone(): lax.all_to_all(jnp.broadcast_to(value[None], (length, *value.shape)), axi...]
    all_to_all x11 -> x14, starting transfers between devices: 64.1 us -> 71.7 us  [from_everyone(): lax.all_to_all(jnp.broadcast_to(value[None], (length, *value.shape)), axi...]
    ppermute x0 -> x60, waiting for transfers between devices: none -> 5.47 us  [the longest x28 5 us: wires_group(): v_now = lax.ppermute(tmp[-1], ax_name, row_list)]
  transfers between devices with their start and end apart: 19 -> 78, of which waited for: 19 -> 13; matrix products, arithmetic and copies ran while one was open for 11% -> 35% of each run, Pallas kernels for 0% -> 0%
where the time goes in v1:
time: 343 us; the launch traced here: 339 us
  starting transfers between devices  155 us (45%)
  local copies, waits for them, and re-layouts  97.5 us (28%)
  waiting for transfers between devices  46.5 us (14%)
  matrix products  21.4 us (6%)
  between operations  14.8 us (4%)
    all_to_all x14, starting transfers between devices, from_everyone(): lax.all_to_all(jnp.broadcast_to(value[None], (length, *value.shape)), axi...  71.7 us
    unnamed x153, local copies, waits for them, and re-layouts  67.4 us
    ppermute x28, starting transfers between devices, wires_group(): v_now = lax.ppermute(tmp[-1], ax_name, row_list)  52.3 us
    all_to_all x14, waiting for transfers between devices, from_everyone(): lax.all_to_all(jnp.broadcast_to(value[None], (length, *value.shape)), axi...  39.1 us
    ppermute x32, starting transfers between devices, wires_group(): reply.append(lax.ppermute(reply[-1], ax_name, entries))  31 us
    dot_general x8, matrix products, times_inverse(): lax.dot_general(block, inverse, (((1,), (1,)), ((), ())), preferred_eleme...  19.6 us
    broadcast_in_dim x19, local copies, waits for them, and re-layouts, from_everyone(): jnp.broadcast_to(value[None], (length, *value.shape))  12.6 us
  transfers between devices with their start and end apart: 78, of which 13 were waited for; matrix products, arithmetic and copies ran while one was open for 35% of the time, Pallas kernels for 0%

profile of v1, /device:TPU:1, one launch (start us, length us, event | category | flops | bytes accessed | tf_op | source)
XLA Modules:
  0.0 338.7 jit_solution(14593260002806433008)
XLA Ops:
  20.4 6.9 %all-to-all-start = ((bf16[16,64,256]{2,1,0:T(8,128)(2,1)}), bf16[16,64,256]{2,1,0:T(8,128)(2,1)S(1)}, u32[]{:S(2)}, u32[]{:S(2)}) async-start(bf16[16,64,256]{2,1,0:T(8,128)(2,1)} %broadcast_in_dim.83), calls=%async_computation | async-start | bytes 1048576 | tf_op jit(solution)/shard_map/all_to_all | solution.py:18
  35.5 3.1 collective-permute-start.23
  50.5 4.5 %collective-permute-start.10 = (bf16[256,256]{1,0:T(8,128)(2,1)S(1)}, bf16[256,256]{1,0:T(8,128)(2,1)}, u32[]{:S(2)}, u32[]{:S(2)}) collective-permute-start(bf16[256,256]{1,0:T(8,128)(2,1)S(1)} %collective-permute-done.9), channel_id=1, source_target_pairs={{0,240},{16,0},{32,16},{48,32},{64,48},{80,64},{96,80},{112,96},{1... | collective-permute-start | bytes 393224 | tf_op jit(solution)/shard_map/ppermute | solution.py:96
  71.3 4.1 %collective-permute-start.24 = (bf16[256,256]{1,0:T(8,128)(2,1)S(1)}, bf16[256,256]{1,0:T(8,128)(2,1)}, u32[]{:S(2)}, u32[]{:S(2)}) collective-permute-start(bf16[256,256]{1,0:T(8,128)(2,1)S(1)} %collective-permute-done.23), channel_id=1, source_target_pairs={{0,240},{16,0},{32,16},{48,32},{64,48},{80,64},{96,80},{112,96},{1... | collective-permute-start | bytes 393224 | tf_op jit(solution)/shard_map/ppermute | solution.py:96
  89.9 6.9 %all-to-all-start.1 = ((bf16[16,3,64,128]{3,2,1,0:T(8,128)(2,1)}), bf16[16,3,64,128]{3,2,1,0:T(8,128)(2,1)S(1)}, u32[]{:S(2)}, u32[]{:S(2)}) async-start(bf16[16,3,64,128]{3,2,1,0:T(8,128)(2,1)} %broadcast_in_dim.85), calls=%async_computation.1 | async-start | bytes 1572864 | tf_op jit(solution)/shard_map/all_to_all | solution.py:18
  111.6 6.7 %all-to-all-start.2 = ((bf16[16,64,256]{2,1,0:T(8,128)(2,1)}), bf16[16,64,256]{2,1,0:T(8,128)(2,1)S(1)}, u32[]{:S(2)}, u32[]{:S(2)}) async-start(bf16[16,64,256]{2,1,0:T(8,128)(2,1)} %broadcast_in_dim.89), calls=%async_computation.2 | async-start | bytes 1048576 | tf_op jit(solution)/shard_map/all_to_all | solution.py:18
  134.3 6.9 %all-to-all-start.3 = ((bf16[16,2,64,128]{3,2,1,0:T(8,128)(2,1)}), bf16[16,2,64,128]{3,2,1,0:T(8,128)(2,1)S(1)}, u32[]{:S(2)}, u32[]{:S(2)}) async-start(bf16[16,2,64,128]{3,2,1,0:T(8,128)(2,1)} %broadcast_in_dim.91), calls=%async_computation.3 | async-start | bytes 1048576 | tf_op jit(solution)/shard_map/all_to_all | solution.py:18
  146.6 6.0 %all-to-all-done.3 = bf16[16,2,64,128]{3,2,1,0:T(8,128)(2,1)S(1)} async-done(((bf16[16,2,64,128]{3,2,1,0:T(8,128)(2,1)}), bf16[16,2,64,128]{3,2,1,0:T(8,128)(2,1)S(1)}, u32[]{:S(2)}, u32[]{:S(2)}) %all-to-all-start.3) | async-done | bytes 524320 | tf_op jit(solution)/shard_map/all_to_all | solution.py:18
  153.7 3.6 %all-to-all-start.4 = ((bf16[16,64,256]{2,1,0:T(8,128)(2,1)}), bf16[16,64,256]{2,1,0:T(8,128)(2,1)S(1)}, u32[]{:S(2)}, u32[]{:S(2)}) async-start(bf16[16,64,256]{2,1,0:T(8,128)(2,1)} %broadcast_in_dim.187), calls=%async_computation.4 | async-start | bytes 1048576 | tf_op jit(solution)/shard_map/all_to_all | solution.py:18
  164.4 3.9 %all-to-all-done.4 = bf16[16,64,256]{2,1,0:T(8,128)(2,1)S(1)} async-done(((bf16[16,64,256]{2,1,0:T(8,128)(2,1)}), bf16[16,64,256]{2,1,0:T(8,128)(2,1)S(1)}, u32[]{:S(2)}, u32[]{:S(2)}) %all-to-all-start.4) | async-done | bytes 524320 | tf_op jit(solution)/shard_map/all_to_all | solution.py:18
  171.7 3.5 %all-to-all-start.5 = ((bf16[16,1,64,128]{3,2,1,0:T(8,128)(2,1)}), bf16[16,1,64,128]{3,2,1,0:T(8,128)(2,1)S(1)}, u32[]{:S(2)}, u32[]{:S(2)}) async-start(bf16[16,1,64,128]{3,2,1,0:T(8,128)(2,1)} %broadcast_in_dim.191), calls=%async_computation.5 | async-start | bytes 524288 | tf_op jit(solution)/shard_map/all_to_all | solution.py:18
  179.2 3.6 %all-to-all-done.5 = bf16[16,1,64,128]{3,2,1,0:T(8,128)(2,1)S(1)} async-done(((bf16[16,1,64,128]{3,2,1,0:T(8,128)(2,1)}), bf16[16,1,64,128]{3,2,1,0:T(8,128)(2,1)S(1)}, u32[]{:S(2)}, u32[]{:S(2)}) %all-to-all-start.5) | async-done | bytes 262176 | tf_op jit(solution)/shard_map/all_to_all | solution.py:18
  183.9 3.6 %all-to-all-start.6 = ((bf16[16,64,256]{2,1,0:T(8,128)(2,1)}), bf16[16,64,256]{2,1,0:T(8,128)(2,1)S(1)}, u32[]{:S(2)}, u32[]{:S(2)}) async-start(bf16[16,64,256]{2,1,0:T(8,128)(2,1)} %broadcast_in_dim.195), calls=%async_computation.6 | async-start | bytes 1048576 | tf_op jit(solution)/shard_map/all_to_all | solution.py:18
  190.4 6.4 %all-to-all-done.6 = bf16[16,64,256]{2,1,0:T(8,128)(2,1)S(1)} async-done(((bf16[16,64,256]{2,1,0:T(8,128)(2,1)}), bf16[16,64,256]{2,1,0:T(8,128)(2,1)S(1)}, u32[]{:S(2)}, u32[]{:S(2)}) %all-to-all-start.6) | async-done | bytes 524320 | tf_op jit(solution)/shard_map/all_to_all | solution.py:18
  200.1 3.6 %all-to-all-start.7 = ((bf16[16,64,256]{2,1,0:T(8,128)(2,1)}), bf16[16,64,256]{2,1,0:T(8,128)(2,1)S(1)}, u32[]{:S(2)}, u32[]{:S(2)}) async-start(bf16[16,64,256]{2,1,0:T(8,128)(2,1)} %broadcast_in_dim.196), calls=%async_computation.7 | async-start | bytes 1048576 | tf_op jit(solution)/shard_map/all_to_all | solution.py:18
  216.4 5.5 %all-to-all-start.8 = ((bf16[16,3,64,128]{3,2,1,0:T(8,128)(2,1)}), bf16[16,3,64,128]{3,2,1,0:T(8,128)(2,1)S(1)}, u32[]{:S(2)}, u32[]{:S(2)}) async-start(bf16[16,3,64,128]{3,2,1,0:T(8,128)(2,1)} %broadcast_in_dim.197), calls=%async_computation.8 | async-start | bytes 1572864 | tf_op jit(solution)/shard_map/all_to_all | solution.py:18
  223.8 3.8 %collective-permute-start.54 = (bf16[256,256]{1,0:T(8,128)(2,1)}, bf16[256,256]{1,0:T(8,128)(2,1)S(1)}, u32[]{:S(2)}, u32[]{:S(2)}) collective-permute-start(bf16[256,256]{1,0:T(8,128)(2,1)} %collective-permute-done.53), channel_id=1, source_target_pairs={{0,240},{16,0},{32,16},{48,32},{64,48},{80,64},{96,80},{112,96},{1... | collective-permute-start | bytes 393224 | tf_op jit(solution)/shard_map/ppermute | solution.py:96
  245.7 6.6 %all-to-all-start.9 = ((bf16[16,64,256]{2,1,0:T(8,128)(2,1)}), bf16[16,64,256]{2,1,0:T(8,128)(2,1)S(1)}, u32[]{:S(2)}, u32[]{:S(2)}) async-start(bf16[16,64,256]{2,1,0:T(8,128)(2,1)} %broadcast_in_dim.202), calls=%async_computation.9 | async-start | bytes 1048576 | tf_op jit(solution)/shard_map/all_to_all | solution.py:18
  266.0 3.7 %all-to-all-start.10 = ((bf16[16,2,64,128]{3,2,1,0:T(8,128)(2,1)}), bf16[16,2,64,128]{3,2,1,0:T(8,128)(2,1)S(1)}, u32[]{:S(2)}, u32[]{:S(2)}) async-start(bf16[16,2,64,128]{3,2,1,0:T(8,128)(2,1)} %broadcast_in_dim.203), calls=%async_computation.10 | async-start | bytes 1048576 | tf_op jit(solution)/shard_map/all_to_all | solution.py:18
  283.5 6.6 %all-to-all-start.11 = ((bf16[16,64,256]{2,1,0:T(8,128)(2,1)}), bf16[16,64,256]{2,1,0:T(8,128)(2,1)S(1)}, u32[]{:S(2)}, u32[]{:S(2)}) async-start(bf16[16,64,256]{2,1,0:T(8,128)(2,1)} %broadcast_in_dim.208), calls=%async_computation.11 | async-start | bytes 1048576 | tf_op jit(solution)/shard_map/all_to_all | solution.py:18
  293.6 6.7 %all-to-all-done.11 = bf16[16,64,256]{2,1,0:T(8,128)(2,1)S(1)} async-done(((bf16[16,64,256]{2,1,0:T(8,128)(2,1)}), bf16[16,64,256]{2,1,0:T(8,128)(2,1)S(1)}, u32[]{:S(2)}, u32[]{:S(2)}) %all-to-all-start.11) | async-done | bytes 524320 | tf_op jit(solution)/shard_map/all_to_all | solution.py:18
  303.7 3.5 %all-to-all-start.12 = ((bf16[16,1,64,128]{3,2,1,0:T(8,128)(2,1)}), bf16[16,1,64,128]{3,2,1,0:T(8,128)(2,1)S(1)}, u32[]{:S(2)}, u32[]{:S(2)}) async-start(bf16[16,1,64,128]{3,2,1,0:T(8,128)(2,1)} %broadcast_in_dim.210), calls=%async_computation.12 | async-start | bytes 524288 | tf_op jit(solution)/shard_map/all_to_all | solution.py:18
  315.8 4.0 %all-to-all-start.13 = ((bf16[16,64,256]{2,1,0:T(8,128)(2,1)}), bf16[16,64,256]{2,1,0:T(8,128)(2,1)S(1)}, u32[]{:S(2)}, u32[]{:S(2)}) async-start(bf16[16,64,256]{2,1,0:T(8,128)(2,1)} %broadcast_in_dim.214), calls=%async_computation.13 | async-start | bytes 1048576 | tf_op jit(solution)/shard_map/all_to_all | solution.py:18
  323.2 5.6 %all-to-all-done.13 = bf16[16,64,256]{2,1,0:T(8,128)(2,1)S(1)} async-done(((bf16[16,64,256]{2,1,0:T(8,128)(2,1)}), bf16[16,64,256]{2,1,0:T(8,128)(2,1)S(1)}, u32[]{:S(2)}, u32[]{:S(2)}) %all-to-all-start.13) | async-done | bytes 524320 | tf_op jit(solution)/shard_map/all_to_all | solution.py:18
  (376 shorter events, 204.3 us)
Async XLA Ops:
  6.5 79.7 %all-gather.9.cloned.1.call-start = ((), (), s32[]{:S(2)}) async-start(), calls=%async_computation.14 | async-start | bytes 2228224 | tf_op jit(solution)/shard_map/all_gather | solution.py:57
  8.5 122.3 %all-gather.11.cloned.1.call-start = ((), (), s32[]{:S(2)}) async-start(), calls=%async_computation.15 | async-start | bytes 2228224 | tf_op jit(solution)/shard_map/all_gather | solution.py:57
  9.3 159.1 %all-gather.13.cloned.1.call-start = ((), (), s32[]{:S(2)}) async-start(), calls=%async_computation.16 | async-start | bytes 2228224 | tf_op jit(solution)/shard_map/all_gather | solution.py:57
  14.9 23.7 %collective-permute-start.8 = (bf16[256,256]{1,0:T(8,128)(2,1)S(1)}, bf16[256,256]{1,0:T(8,128)(2,1)S(1)}, u32[]{:S(2)}, u32[]{:S(2)}) collective-permute-start(bf16[256,256]{1,0:T(8,128)(2,1)S(1)} %get-tuple-element.150), channel_id=1, source_target_pairs={{0,240},{16,0},{32,16},{48,32},{64,48},{80,64},{96,80},{112,96},{1... | collective-permute-start | bytes 393224 | tf_op jit(solution)/shard_map/ppermute | solution.py:96
  20.4 50.8 %all-to-all-start = ((bf16[16,64,256]{2,1,0:T(8,128)(2,1)}), bf16[16,64,256]{2,1,0:T(8,128)(2,1)S(1)}, u32[]{:S(2)}, u32[]{:S(2)}) async-start(bf16[16,64,256]{2,1,0:T(8,128)(2,1)} %broadcast_in_dim.83), calls=%async_computation | async-start | bytes 1048576 | tf_op jit(solution)/shard_map/all_to_all | solution.py:18
  27.2 169.6 %all-gather.15.cloned.1.call-start = ((), (), s32[]{:S(2)}) async-start(), calls=%async_computation.17 | async-start | bytes 2228224 | tf_op jit(solution)/shard_map/all_gather | solution.py:57
  71.3 26.9 %collective-permute-start.24 = (bf16[256,256]{1,0:T(8,128)(2,1)S(1)}, bf16[256,256]{1,0:T(8,128)(2,1)}, u32[]{:S(2)}, u32[]{:S(2)}) collective-permute-start(bf16[256,256]{1,0:T(8,128)(2,1)S(1)} %collective-permute-done.23), channel_id=1, source_target_pairs={{0,240},{16,0},{32,16},{48,32},{64,48},{80,64},{96,80},{112,96},{1... | collective-permute-start | bytes 393224 | tf_op jit(solution)/shard_map/ppermute | solution.py:96
  75.4 23.5 %collective-permute-start.12 = (bf16[256,256]{1,0:T(8,128)(2,1)}, bf16[256,256]{1,0:T(8,128)(2,1)}, u32[]{:S(2)}, u32[]{:S(2)}) collective-permute-start(bf16[256,256]{1,0:T(8,128)(2,1)} %collective-permute-done.11), channel_id=1, source_target_pairs={{0,240},{16,0},{32,16},{48,32},{64,48},{80,64},{96,80},{112,96},{1... | collective-permute-start | bytes 393224 | tf_op jit(solution)/shard_map/ppermute | solution.py:96
  78.4 23.2 %collective-permute-start.5 = (bf16[256,256]{1,0:T(8,128)(2,1)}, bf16[256,256]{1,0:T(8,128)(2,1)}, u32[]{:S(2)}, u32[]{:S(2)}) collective-permute-start(bf16[256,256]{1,0:T(8,128)(2,1)} %collective-permute-done.4), channel_id=1, source_target_pairs={{0,16},{16,32},{32,48},{48,64},{64,80},{80,96},{96,112},{112,128},... | collective-permute-start | bytes 393224 | tf_op jit(solution)/shard_map/ppermute | solution.py:94
  78.4 24.0 %collective-permute-start.51 = (bf16[256,256]{1,0:T(8,128)(2,1)}, bf16[256,256]{1,0:T(8,128)(2,1)}, u32[]{:S(2)}, u32[]{:S(2)}) collective-permute-start(bf16[256,256]{1,0:T(8,128)(2,1)} %collective-permute-done.50), channel_id=1, source_target_pairs={{0,16},{16,32},{32,48},{48,64},{64,80},{80,96},{96,112},{112,128},... | collective-permute-start | bytes 393224 | tf_op jit(solution)/shard_map/ppermute | solution.py:94
  78.4 25.0 %collective-permute-start.37 = (bf16[256,256]{1,0:T(8,128)(2,1)}, bf16[256,256]{1,0:T(8,128)(2,1)}, u32[]{:S(2)}, u32[]{:S(2)}) collective-permute-start(bf16[256,256]{1,0:T(8,128)(2,1)} %collective-permute-done.36), channel_id=1, source_target_pairs={{0,16},{16,32},{32,48},{48,64},{64,80},{80,96},{96,112},{112,128},... | collective-permute-start | bytes 393224 | tf_op jit(solution)/shard_map/ppermute | solution.py:94
  98.2 23.9 %collective-permute-start.38 = (bf16[256,256]{1,0:T(8,128)(2,1)}, bf16[256,256]{1,0:T(8,128)(2,1)}, u32[]{:S(2)}, u32[]{:S(2)}) collective-permute-start(bf16[256,256]{1,0:T(8,128)(2,1)} %copy-done.39), channel_id=1, source_target_pairs={{0,240},{16,0},{32,16},{48,32},{64,48},{80,64},{96,80},{112,96},{1... | collective-permute-start | bytes 393224 | tf_op jit(solution)/shard_map/ppermute | solution.py:96
  98.9 23.9 %collective-permute-start.25 = (bf16[256,256]{1,0:T(8,128)(2,1)}, bf16[256,256]{1,0:T(8,128)(2,1)}, u32[]{:S(2)}, u32[]{:S(2)}) collective-permute-start(bf16[256,256]{1,0:T(8,128)(2,1)} %collective-permute-done.24), channel_id=1, source_target_pairs={{0,240},{16,0},{32,16},{48,32},{64,48},{80,64},{96,80},{112,96},{1... | collective-permute-start | bytes 393224 | tf_op jit(solution)/shard_map/ppermute | solution.py:96
  101.6 23.5 %collective-permute-start.13 = (bf16[256,256]{1,0:T(8,128)(2,1)}, bf16[256,256]{1,0:T(8,128)(2,1)}, u32[]{:S(2)}, u32[]{:S(2)}) collective-permute-start(bf16[256,256]{1,0:T(8,128)(2,1)} %collective-permute-done.12), channel_id=1, source_target_pairs={{0,240},{16,0},{32,16},{48,32},{64,48},{80,64},{96,80},{112,96},{1... | collective-permute-start | bytes 393224 | tf_op jit(solution)/shard_map/ppermute | solution.py:96
  102.4 23.5 %collective-permute-start.6 = (bf16[256,256]{1,0:T(8,128)(2,1)}, bf16[256,256]{1,0:T(8,128)(2,1)}, u32[]{:S(2)}, u32[]{:S(2)}) collective-permute-start(bf16[256,256]{1,0:T(8,128)(2,1)} %collective-permute-done.5), channel_id=1, source_target_pairs={{0,16},{16,32},{32,48},{48,64},{64,80},{80,96},{96,112},{112,128},... | collective-permute-start | bytes 393224 | tf_op jit(solution)/shard_map/ppermute | solution.py:94
  122.1 101.7 %collective-permute-start.53 = (bf16[256,256]{1,0:T(8,128)(2,1)}, bf16[256,256]{1,0:T(8,128)(2,1)}, u32[]{:S(2)}, u32[]{:S(2)}) collective-permute-start(bf16[256,256]{1,0:T(8,128)(2,1)} %copy-done.38), channel_id=1, source_target_pairs={{0,240},{16,0},{32,16},{48,32},{64,48},{80,64},{96,80},{112,96},{1... | collective-permute-start | bytes 393224 | tf_op jit(solution)/shard_map/ppermute | solution.py:96
  122.9 104.8 %collective-permute-start.39 = (bf16[256,256]{1,0:T(8,128)(2,1)}, bf16[256,256]{1,0:T(8,128)(2,1)}, u32[]{:S(2)}, u32[]{:S(2)}) collective-permute-start(bf16[256,256]{1,0:T(8,128)(2,1)} %collective-permute-done.38), channel_id=1, source_target_pairs={{0,240},{16,0},{32,16},{48,32},{64,48},{80,64},{96,80},{112,96},{1... | collective-permute-start | bytes 393224 | tf_op jit(solution)/shard_map/ppermute | solution.py:96
  125.1 102.7 %collective-permute-start.26 = (bf16[256,256]{1,0:T(8,128)(2,1)}, bf16[256,256]{1,0:T(8,128)(2,1)}, u32[]{:S(2)}, u32[]{:S(2)}) collective-permute-start(bf16[256,256]{1,0:T(8,128)(2,1)} %collective-permute-done.25), channel_id=1, source_target_pairs={{0,240},{16,0},{32,16},{48,32},{64,48},{80,64},{96,80},{112,96},{1... | collective-permute-start | bytes 393224 | tf_op jit(solution)/shard_map/ppermute | solution.py:96
  125.9 84.1 %collective-permute-start.14 = (bf16[256,256]{1,0:T(8,128)(2,1)}, bf16[256,256]{1,0:T(8,128)(2,1)}, u32[]{:S(2)}, u32[]{:S(2)}) collective-permute-start(bf16[256,256]{1,0:T(8,128)(2,1)} %collective-permute-done.13), channel_id=1, source_target_pairs={{0,240},{16,0},{32,16},{48,32},{64,48},{80,64},{96,80},{112,96},{1... | collective-permute-start | bytes 393224 | tf_op jit(solution)/shard_map/ppermute | solution.py:96
  125.9 32.1 %collective-permute-start.7 = (bf16[256,256]{1,0:T(8,128)(2,1)}, bf16[256,256]{1,0:T(8,128)(2,1)}, u32[]{:S(2)}, u32[]{:S(2)}) collective-permute-start(bf16[256,256]{1,0:T(8,128)(2,1)} %collective-permute-done.6), channel_id=1, source_target_pairs={{0,16},{16,32},{32,48},{48,64},{64,80},{80,96},{96,112},{112,128},... | collective-permute-start | bytes 393224 | tf_op jit(solution)/shard_map/ppermute | solution.py:94
  216.4 28.0 %all-to-all-start.8 = ((bf16[16,3,64,128]{3,2,1,0:T(8,128)(2,1)}), bf16[16,3,64,128]{3,2,1,0:T(8,128)(2,1)S(1)}, u32[]{:S(2)}, u32[]{:S(2)}) async-start(bf16[16,3,64,128]{3,2,1,0:T(8,128)(2,1)} %broadcast_in_dim.197), calls=%async_computation.8 | async-start | bytes 1572864 | tf_op jit(solution)/shard_map/all_to_all | solution.py:18
  236.6 33.8 %collective-permute-start.56 = (bf16[256,256]{1,0:T(8,128)(2,1)S(1)}, bf16[256,256]{1,0:T(8,128)(2,1)S(1)}, u32[]{:S(2)}, u32[]{:S(2)}) collective-permute-start(bf16[256,256]{1,0:T(8,128)(2,1)S(1)} %collective-permute-done.55), channel_id=1, source_target_pairs={{0,240},{16,0},{32,16},{48,32},{64,48},{80,64},{96,80},{112,96},{1... | collective-permute-start | bytes 393224 | tf_op jit(solution)/shard_map/ppermute | solution.py:96
  238.0 34.8 %collective-permute-start.42 = (bf16[256,256]{1,0:T(8,128)(2,1)S(1)}, bf16[256,256]{1,0:T(8,128)(2,1)S(1)}, u32[]{:S(2)}, u32[]{:S(2)}) collective-permute-start(bf16[256,256]{1,0:T(8,128)(2,1)S(1)} %collective-permute-done.41), channel_id=1, source_target_pairs={{0,240},{16,0},{32,16},{48,32},{64,48},{80,64},{96,80},{112,96},{1... | collective-permute-start | bytes 393224 | tf_op jit(solution)/shard_map/ppermute | solution.py:96
  274.8 32.5 %collective-permute-start.58 = (bf16[256,256]{1,0:T(8,128)(2,1)S(1)}, bf16[256,256]{1,0:T(8,128)(2,1)S(1)}, u32[]{:S(2)}, u32[]{:S(2)}) collective-permute-start(bf16[256,256]{1,0:T(8,128)(2,1)S(1)} %collective-permute-done.57), channel_id=1, source_target_pairs={{0,240},{16,0},{32,16},{48,32},{64,48},{80,64},{96,80},{112,96},{1... | collective-permute-start | bytes 393224 | tf_op jit(solution)/shard_map/ppermute | solution.py:96
  (102 other events, 1513.9 us)
Sparse Core Ops, SparseCore 0:
  9.1 50.0 all-gather.8
  61.0 40.6 all-gather.10
  103.4 41.0 all-gather.12
  146.1 40.7 all-gather.14
